TPU v7x, 512 devices: a whole 4x8x8 slice. The times are simulated.
512 devices in a mesh: slab: 16 (over z, core), sub: 32 (over y, x).
Axes of the slice: x: 4, y: 8, z: 8, core: 2. Of those that a mesh axis runs over, the one named last changes fastest.
Arguments:
- velocity_field: float32 [3, 256, 1024, 512], P(None, 'slab', 'sub'), may hold values from -6 to 6
- particle_state: float32 [16384, 6, 256], P(('slab', 'sub')), as said below
- stokes_time: float32 [16384, 256], P(('slab', 'sub')), may hold values from 0.2 to 2
- box_base: int32 [16384, 3], P(('slab', 'sub')), may hold values from -2 to 511, as said below
- live_bins: int32 [512], P(('slab', 'sub')), may hold values from 1 to 32, as said below
Outputs:
- state_out: float32 [16384, 6, 256], P(('slab', 'sub'))
Inputs may be any that keep to these rules, and one draw needn't show every extreme that they name: `box_base`: columns 0 and 1 lie from -2 to 14 and from -2 to 30, column 2 from 0 to 511; bin 0 has column 0 at -2 and column 2 at 511. `live_bins`: some device has all 32 slots occupied. `particle_state`: positions lie in the box's central cell, 0 to 1 in each coordinate.
All inputs are finite; a program needn't handle non-finite values.
Results may differ from a plain program's by a relative error of at most 0.0003.
Values sent between devices are 32-bit elements; how exact they have to be, the bound alone decides.
A program may use at most 64 MiB of HBM per device.

v0:
```python
import functools

import jax
import jax.numpy as jnp
from jax import lax
from jax.experimental import pallas as pl
from jax.experimental.pallas import tpu as pltpu
from jax.sharding import PartitionSpec as P

SUBSTEPS = 4
STEP_SIZE = 0.2
WIDTH = 2
LANES = 128
TOP = 8
ROWS = 8
LINES = 48
MESH = pl.DeviceIdType.MESH

POWERS = (
    (0.0, 1.0, 0.0, 0.0),
    (-1 / 3, -1 / 2, 1.0, -1 / 6),
    (1 / 2, -1.0, 1 / 2, 0.0),
    (-1 / 6, 1 / 2, -1 / 2, 1 / 6),
)


def power_matrix(shape, power, node, same):
    out = jnp.zeros(shape, jnp.float32)
    for p in range(4):
        for n in range(4):
            if POWERS[p][n]:
                out = jnp.where((power == p) & (node == n) & same, POWERS[p][n], out)
    return out


def dot(a, b):
    return jnp.dot(a, b, precision=lax.Precision.HIGHEST, preferred_element_type=jnp.float32)


def sample(factor, position):
    x, y, z = position
    count = len(x)
    velocity = []
    for c in range(3):
        over_x = None
        for i in (3, 2, 1, 0):
            over_y = None
            for j in (3, 2, 1, 0):
                line = ((c * 4 + i) * 4 + j) * 4
                over_z = [factor(line + 3)] * count
                for k in (2, 1, 0):
                    f = factor(line + k)
                    over_z = [over_z[n] * z[n] + f for n in range(count)]
                over_y = over_z if over_y is None else [over_y[n] * y[n] + over_z[n] for n in range(count)]
            over_x = over_y if over_x is None else [over_x[n] * x[n] + over_y[n] for n in range(count)]
        velocity.append(over_x)
    return velocity


def kernel(n_slab, n_sub, field, states, stokes, bases, live, out,
           padded, parts, moved, picked, turned, factors, local_sems, part_sems, out_sems, send_sems, recv_sems):
    g, s = lax.axis_index("slab"), lax.axis_index("sub")
    _, cx, cy, nz = field.shape
    tiles = nz // LANES
    bins, _, part = states.shape

    loads = []
    for t in range(tiles):
        loads.append(
            pltpu.make_async_copy(
                field.at[:, :, :, pl.ds(t * LANES, LANES)],
                padded.at[:, pl.ds(WIDTH, cx), t, pl.ds(TOP, cy), :],
                local_sems.at[t],
            )
        )
        loads[-1].start()
    for q in range(6):
        loads.append(pltpu.make_async_copy(states.at[:, q, :], parts.at[q], part_sems.at[q]))
        loads[-1].start()

    steps = [(dx, dy) for dx in (-1, 1) for dy in (-1, 1)] + [(0, -1), (0, 1), (-1, 0), (1, 0)]

    def peer(dx, dy):
        return (lax.rem(g + dx + n_slab, n_slab), lax.rem(s + dy + n_sub, n_sub))

    barrier = pltpu.get_barrier_semaphore()
    for dx, dy in steps:
        pl.semaphore_signal(barrier, inc=1, device_id=peer(dx, dy), device_id_type=MESH)
    pl.semaphore_wait(barrier, len(steps))

    def source(d, n):
        return {-1: (0, WIDTH), 0: (0, n), 1: (n - WIDTH, WIDTH)}[d]

    def target(d, n, origin):
        return {-1: (origin + n, WIDTH), 0: (origin, n), 1: (origin - WIDTH, WIDTH)}[d]

    halo = []
    for k, (dx, dy) in enumerate(steps):
        for t in range(tiles):
            (x0, xn), (y0, yn) = source(dx, cx), source(dy, cy)
            (u0, un), (w0, wn) = target(dx, cx, WIDTH), target(dy, cy, TOP)
            copy = pltpu.make_async_remote_copy(
                src_ref=field.at[:, pl.ds(x0, xn), pl.ds(y0, yn), pl.ds(t * LANES, LANES)],
                dst_ref=padded.at[:, pl.ds(u0, un), t, pl.ds(w0, wn), :],
                send_sem=send_sems.at[k, t],
                recv_sem=recv_sems.at[k, t],
                device_id=peer(dx, dy),
                device_id_type=MESH,
            )
            copy.start()
            halo.append(copy)

    row = lax.broadcasted_iota(jnp.int32, (LINES, LINES), 0)
    col = lax.broadcasted_iota(jnp.int32, (LINES, LINES), 1)
    along_y = power_matrix((LINES, LINES), row % 4, col % 4, row // 4 == col // 4)
    along_x = power_matrix((LINES, LINES), row // 4 % 4, col // 4 % 4, (row // 16 == col // 16) & (row % 4 == col % 4))
    along_xy = dot(along_x, along_y)
    zr = lax.broadcasted_iota(jnp.int32, (LANES, LANES), 0)
    zc = lax.broadcasted_iota(jnp.int32, (LANES, LANES), 1)
    along_z = power_matrix((LANES, LANES), zc % 4, zr % 4, zr // 4 == zc // 4)

    for copy in loads:
        copy.wait()
    for copy in halo:
        copy.wait()

    lane = lax.broadcasted_iota(jnp.int32, (4, LANES), 1)
    for b in range(bins):
        x0, y0, z0 = bases[0, b] + WIDTH, bases[1, b] + TOP, bases[2, b]
        here = z0 // LANES
        after = lax.rem(here + 1, tiles)
        first = lane >= lax.rem(z0, LANES)
        for c in range(3):
            for i in range(4):
                a = padded[c, x0 + i, here, pl.ds(y0, 4), :]
                n = padded[c, x0 + i, after, pl.ds(y0, 4), :]
                picked[b, pl.ds((c * 4 + i) * 4, 4), :] = jnp.where(first, a, n)

    wide = lax.broadcasted_iota(jnp.int32, (LINES, LANES), 1)
    boxes = jnp.zeros((LINES, LANES), jnp.float32)
    for b in range(bins):
        shift = lax.rem(4 * b + LANES - lax.rem(bases[2, b], LANES), LANES)
        boxes = jnp.where(wide // 4 == b, pltpu.roll(picked[b], shift, 1), boxes)
    boxes = dot(dot(along_xy, boxes), along_z)
    turned[:, pl.ds(0, LINES)] = boxes.T

    for group in range(bins // ROWS):
        for k in range(4):
            v = turned[pl.ds(group * ROWS * 4 + k, ROWS, stride=4), :]
            for n in range(LINES):
                factors[group, n * 4 + k] = jnp.broadcast_to(v[:, n : n + 1], (ROWS, LANES))

    halves = [pl.ds(h * LANES, LANES) for h in range(part // LANES)]

    @pl.loop(0, bins // ROWS)
    def _(group):
        rows = pl.ds(pl.multiple_of(group * ROWS, ROWS), ROWS)
        start = [[parts[q, rows, h] for h in halves] for q in range(6)]
        rate = [1.0 / stokes[rows, h] for h in halves]
        keep = group * ROWS + lax.broadcasted_iota(jnp.int32, (ROWS, LANES), 0) < live[0]
        factor = lambda n: factors[group, n]
        span = range(len(halves))

        def substep(_, state):
            x, v = state[:3], state[3:]
            u = sample(factor, x)
            a = [[(u[c][h] - v[c][h]) * rate[h] for h in span] for c in range(3)]
            xm = [[x[c][h] + 0.5 * STEP_SIZE * v[c][h] for h in span] for c in range(3)]
            vm = [[v[c][h] + 0.5 * STEP_SIZE * a[c][h] for h in span] for c in range(3)]
            x = [[x[c][h] + STEP_SIZE * vm[c][h] for h in span] for c in range(3)]
            um = sample(factor, xm)
            v = [[v[c][h] + STEP_SIZE * (um[c][h] - vm[c][h]) * rate[h] for h in span] for c in range(3)]
            return x + v

        end = lax.fori_loop(0, SUBSTEPS, substep, start)
        for q in range(6):
            for h in span:
                moved[q, rows, halves[h]] = jnp.where(keep, end[q][h], start[q][h])

    stores = []
    for q in range(6):
        stores.append(pltpu.make_async_copy(moved.at[q], out.at[:, q, :], out_sems.at[q]))
        stores[-1].start()
    for copy in stores:
        copy.wait()


def body(velocity_field, particle_state, stokes_time, box_base, live_bins):
    n_slab, n_sub = lax.axis_size("slab"), lax.axis_size("sub")
    _, cx, cy, nz = velocity_field.shape
    tiles = nz // LANES
    bins, _, part = particle_state.shape
    anywhere = pl.BlockSpec(memory_space=pl.ANY)
    vmem = pl.BlockSpec(memory_space=pltpu.VMEM)
    smem = pl.BlockSpec(memory_space=pltpu.SMEM)
    return pl.pallas_call(
        functools.partial(kernel, n_slab, n_sub),
        out_shape=jax.ShapeDtypeStruct(particle_state.shape, jnp.float32),
        in_specs=[anywhere, anywhere, vmem, smem, smem],
        out_specs=anywhere,
        scratch_shapes=[
            pltpu.VMEM((3, cx + 2 * WIDTH, tiles, cy + 2 * TOP, LANES), jnp.float32),
            pltpu.VMEM((6, bins, part), jnp.float32),
            pltpu.VMEM((6, bins, part), jnp.float32),
            pltpu.VMEM((bins, LINES, LANES), jnp.float32),
            pltpu.VMEM((LANES, LANES), jnp.float32),
            pltpu.VMEM((bins // ROWS, LINES * 4, ROWS, LANES), jnp.float32),
            pltpu.SemaphoreType.DMA((tiles,)),
            pltpu.SemaphoreType.DMA((6,)),
            pltpu.SemaphoreType.DMA((6,)),
            pltpu.SemaphoreType.DMA((8, tiles)),
            pltpu.SemaphoreType.DMA((8, tiles)),
        ],
        compiler_params=pltpu.CompilerParams(collective_id=0, has_side_effects=True),
        name="particles",
    )(velocity_field, particle_state, stokes_time, box_base.T, live_bins)


def solution(mesh):
    placed = (
        P(None, "slab", "sub", None),
        P(("slab", "sub"), None, None),
        P(("slab", "sub"), None),
        P(("slab", "sub"), None),
        P(("slab", "sub")),
    )
    return jax.shard_map(
        body, mesh=mesh, in_specs=placed, out_specs=P(("slab", "sub"), None, None), check_vma=False
    )
```

profile of v0, /device:TPU:40, one launch (start us, length us, event | category | flops | bytes accessed | tf_op | source)
XLA Modules:
  0.0 31.8 jit_solution(16352427785538296698)
XLA Ops:
  0.7 1.7 %copy.6.states = f32[32,6,256]{2,1,0:T(8,128)} copy(f32[32,6,256]{2,0,1:T(8,128)} %param.6) | data formatting | bytes 393216 | tf_op args[1]
  2.4 27.7 %particles.1 = f32[32,6,256]{2,1,0:T(8,128)} custom-call(f32[3,16,32,512]{3,2,1,0:T(8,128)} %field.1, f32[32,6,256]{2,1,0:T(8,128)} %copy.6.states, f32[32,256]{1,0:T(8,128)} %stokes.1, s32[3,32]{1,0:T(4,128)} %bitcast.1, s32[1]{0:T(128)S(6)} %copy.8.live), custom_call_target="tpu_custom_call" | custom-call | tf_op jit(solution)/shard_map/particles/pallas_call | solution.py:196
  30.1 1.7 %copy.7 = f32[32,6,256]{2,0,1:T(8,128)} copy(f32[32,6,256]{2,1,0:T(8,128)} %particles.1) | data formatting | bytes 393216 | tf_op jit(solution)/shard_map/particles/pallas_call | solution.py:196
where the time goes:
time: 32 us; the launch traced here: 31.8 us
  Pallas kernels  27.7 us (87%)
  local copies, waits for them, and re-layouts  3.43 us (11%)
  between operations  0.66 us (2%)
    pallas_call x1, Pallas kernels, body(): pl.pallas_call(functools.partial(kernel, n_slab, n_sub), out_shape=jax.Sh...  27.7 us
    unnamed x1, local copies, waits for them, and re-layouts  1.74 us
    pallas_call x1, local copies, waits for them, and re-layouts, body(): pl.pallas_call(functools.partial(kernel, n_slab, n_sub), out_shape=jax.Sh...  1.69 us

commit v1 on v0

v1 whole, which is shorter than its diff:
```python
import functools

import jax
import jax.numpy as jnp
from jax import lax
from jax.experimental import pallas as pl
from jax.experimental.pallas import tpu as pltpu
from jax.sharding import PartitionSpec as P

SUBSTEPS = 4
STEP_SIZE = 0.2
WIDTH = 2
LANES = 128
TOP = 8
LINES = 48
HALF = 16
MESH = pl.DeviceIdType.MESH

POWERS = (
    (-1 / 16, 9 / 16, 9 / 16, -1 / 16),
    (1 / 24, -9 / 8, 9 / 8, -1 / 24),
    (1 / 4, -1 / 4, -1 / 4, 1 / 4),
    (-1 / 6, 1 / 2, -1 / 2, 1 / 6),
)


def power_matrix(shape, power, node, same):
    out = jnp.zeros(shape, jnp.float32)
    for p in range(4):
        for n in range(4):
            out = jnp.where((power == p) & (node == n) & same, POWERS[p][n], out)
    return out


def exact_dot(a, b):
    return jnp.dot(a, b, precision=lax.Precision.HIGHEST, preferred_element_type=jnp.float32)


def split(a):
    high = a.astype(jnp.bfloat16)
    return high, (a - high.astype(jnp.float32)).astype(jnp.bfloat16)


def dot(a, b):
    return jnp.dot(a, b, preferred_element_type=jnp.float32)


def sample(high_box, low_box, position):
    x, y, z = position
    y2, z2 = y * y, z * z
    along_z = [None, z, z2, z2 * z]
    along_y = [None, y, y2, y2 * y]
    terms = []
    for a in along_y:
        for b in along_z:
            terms.append(jnp.ones_like(x) if a is None and b is None else a if b is None else b if a is None else a * b)
    high, low = split(jnp.concatenate(terms, axis=0))
    slices = dot(high_box, high) + dot(low_box, high) + dot(high_box, low)
    velocity = []
    for c in range(3):
        i = [slices[(c * 4 + i) * HALF : (c * 4 + i + 1) * HALF] for i in range(4)]
        velocity.append(((i[3] * x + i[2]) * x + i[1]) * x + i[0])
    return velocity


def kernel(n_slab, n_sub, field, states, stokes, bases_in, live, out,
           padded, parts, rates, moved, picked, planes, boxes_high, boxes_low, bases,
           local_sems, part_sems, out_sem, send_sems, recv_sems):
    comm = n_slab > 1
    _, cx, cy, nz = field.shape
    tiles = nz // LANES
    _, bins, part = states.shape

    loads = []
    for t in range(tiles):
        loads.append(
            pltpu.make_async_copy(
                field.at[:, :, :, pl.ds(t * LANES, LANES)],
                padded.at[:, pl.ds(WIDTH, cx), t, pl.ds(TOP, cy), :],
                local_sems.at[t],
            )
        )
    for n, (here, there) in enumerate(((states, parts), (stokes, rates), (bases_in, bases))):
        loads.append(pltpu.make_async_copy(here, there, part_sems.at[n]))
    for copy in loads:
        copy.start()

    halo = []
    if comm:
        g, s = lax.axis_index("slab"), lax.axis_index("sub")
        steps = [(dx, dy) for dx in (-1, 1) for dy in (-1, 1)] + [(0, -1), (0, 1), (-1, 0), (1, 0)]

        def peer(dx, dy):
            return (lax.rem(g + dx + n_slab, n_slab), lax.rem(s + dy + n_sub, n_sub))

        barrier = pltpu.get_barrier_semaphore()
        for dx, dy in steps:
            pl.semaphore_signal(barrier, inc=1, device_id=peer(dx, dy), device_id_type=MESH)
        pl.semaphore_wait(barrier, len(steps))

        def source(d, n):
            return {-1: (0, WIDTH), 0: (0, n), 1: (n - WIDTH, WIDTH)}[d]

        def target(d, n, origin):
            return {-1: (origin + n, WIDTH), 0: (origin, n), 1: (origin - WIDTH, WIDTH)}[d]

        for k, (dx, dy) in enumerate(steps):
            for t in range(tiles):
                (x0, xn), (y0, yn) = source(dx, cx), source(dy, cy)
                (u0, un), (w0, wn) = target(dx, cx, WIDTH), target(dy, cy, TOP)
                copy = pltpu.make_async_remote_copy(
                    src_ref=field.at[:, pl.ds(x0, xn), pl.ds(y0, yn), pl.ds(t * LANES, LANES)],
                    dst_ref=padded.at[:, pl.ds(u0, un), t, pl.ds(w0, wn), :],
                    send_sem=send_sems.at[k, t],
                    recv_sem=recv_sems.at[k, t],
                    device_id=peer(dx, dy),
                    device_id_type=MESH,
                )
                copy.start()
                halo.append(copy)

    row = lax.broadcasted_iota(jnp.int32, (LINES, LINES), 0)
    col = lax.broadcasted_iota(jnp.int32, (LINES, LINES), 1)
    along_y = power_matrix((LINES, LINES), row % 4, col % 4, row // 4 == col // 4)
    along_x = power_matrix((LINES, LINES), row // 4 % 4, col // 4 % 4, (row // 16 == col // 16) & (row % 4 == col % 4))
    along_xy = exact_dot(along_x, along_y)
    zr = lax.broadcasted_iota(jnp.int32, (LANES, LANES), 0)
    zc = lax.broadcasted_iota(jnp.int32, (LANES, LANES), 1)
    along_z = [
        power_matrix((LANES, LANES), zc // HALF % 4, zr % 4, zr // 4 == zc % HALF + q * HALF) for q in range(bins // HALF)
    ]

    for copy in loads:
        copy.wait()
    parts[0:3] = parts[0:3] - 0.5
    rates[...] = 1.0 / rates[...]
    moved[...] = parts[...]
    for copy in halo:
        copy.wait()

    lane = lax.broadcasted_iota(jnp.int32, (4, LANES), 1)
    for b in range(bins):
        x0, y0, z0 = bases[0, b] + WIDTH, bases[1, b] + TOP, bases[2, b]
        here = z0 // LANES
        after = lax.rem(here + 1, tiles)
        first = lane >= lax.rem(z0, LANES)
        for c in range(3):
            for i in range(4):
                a = padded[c, x0 + i, here, pl.ds(y0, 4), :]
                n = padded[c, x0 + i, after, pl.ds(y0, 4), :]
                picked[b, pl.ds((c * 4 + i) * 4, 4), :] = jnp.where(first, a, n)

    wide = lax.broadcasted_iota(jnp.int32, (LINES, LANES), 1)
    boxes = jnp.zeros((LINES, LANES), jnp.float32)
    for b in range(bins):
        shift = lax.rem(4 * b + LANES - lax.rem(bases[2, b], LANES), LANES)
        boxes = jnp.where(wide // 4 == b, pltpu.roll(picked[b], shift, 1), boxes)
    boxes = exact_dot(along_xy, boxes)
    own = lax.broadcasted_iota(jnp.int32, (HALF, LANES), 0) == lax.broadcasted_iota(jnp.int32, (HALF, LANES), 1) % HALF
    low_lane = lax.broadcasted_iota(jnp.int32, (HALF, LANES), 1) < LANES // 2
    for q in range(bins // HALF):
        planes[q] = exact_dot(boxes, along_z[q])
        for line in range(12):
            for side in range(2):
                j = 2 * side
                even = jnp.broadcast_to(planes[q, pl.ds(line * 4 + j, 1), :], (HALF, LANES))
                odd = jnp.broadcast_to(planes[q, pl.ds(line * 4 + j + 1, 1), :], (HALF, LANES))
                high, low = split(jnp.where(own, jnp.where(low_lane, even, odd), 0.0))
                at = (q, pl.ds(line * HALF, HALF), pl.ds(side * LANES, LANES))
                boxes_high[at] = high
                boxes_low[at] = low

    halves = range(bins // HALF)

    def substep(_, carry):
        state = []
        for q in halves:
            rows = pl.ds(q * HALF, HALF)
            state.append(([moved[c, rows] for c in range(3)], [moved[c + 3, rows] for c in range(3)], rates[rows]))
        u = [sample(boxes_high[q], boxes_low[q], state[q][0]) for q in halves]
        mid = []
        for q in halves:
            x, v, rate = state[q]
            vm = [v[c] + (0.5 * STEP_SIZE) * (u[q][c] - v[c]) * rate for c in range(3)]
            mid.append(([x[c] + (0.5 * STEP_SIZE) * v[c] for c in range(3)], vm))
        um = [sample(boxes_high[q], boxes_low[q], mid[q][0]) for q in halves]
        for q in halves:
            rows = pl.ds(q * HALF, HALF)
            x, v, rate = state[q]
            vm = mid[q][1]
            for c in range(3):
                moved[c, rows] = x[c] + STEP_SIZE * vm[c]
                moved[c + 3, rows] = v[c] + STEP_SIZE * (um[q][c] - vm[c]) * rate
        return carry

    lax.fori_loop(0, SUBSTEPS, substep, 0)
    keep = lax.broadcasted_iota(jnp.int32, (bins, part), 0) < live[0]
    for c in range(6):
        end = jnp.where(keep, moved[c], parts[c])
        moved[c] = end + 0.5 if c < 3 else end
    store = pltpu.make_async_copy(moved, out, out_sem)
    store.start()
    store.wait()


def body(velocity_field, particle_state, stokes_time, box_base, live_bins):
    n_slab, n_sub = lax.axis_size("slab"), lax.axis_size("sub")
    _, cx, cy, nz = velocity_field.shape
    tiles = nz // LANES
    bins, _, part = particle_state.shape
    hbm = pl.BlockSpec(memory_space=pltpu.HBM)
    by_row = (1, 0, 2)
    out = pl.pallas_call(
        functools.partial(kernel, n_slab, n_sub),
        out_shape=jax.ShapeDtypeStruct((6, bins, part), jnp.float32),
        in_specs=[hbm] * 4 + [pl.BlockSpec(memory_space=pltpu.SMEM)],
        out_specs=pl.BlockSpec(memory_space=pl.ANY),
        scratch_shapes=[
            pltpu.VMEM((3, cx + 2 * WIDTH, tiles, cy + 2 * TOP, LANES), jnp.float32),
            pltpu.VMEM((6, bins, part), jnp.float32),
            pltpu.VMEM((bins, part), jnp.float32),
            pltpu.VMEM((6, bins, part), jnp.float32),
            pltpu.VMEM((bins, LINES, LANES), jnp.float32),
            pltpu.VMEM((bins // HALF, LINES, LANES), jnp.float32),
            pltpu.VMEM((bins // HALF, 12 * HALF, 2 * LANES), jnp.bfloat16),
            pltpu.VMEM((bins // HALF, 12 * HALF, 2 * LANES), jnp.bfloat16),
            pltpu.SMEM((3, bins), jnp.int32),
            pltpu.SemaphoreType.DMA((tiles,)),
            pltpu.SemaphoreType.DMA((3,)),
            pltpu.SemaphoreType.DMA,
            pltpu.SemaphoreType.DMA((8, tiles)),
            pltpu.SemaphoreType.DMA((8, tiles)),
        ],
        compiler_params=pltpu.CompilerParams(
            collective_id=0 if n_slab > 1 else None, has_side_effects=True, vmem_limit_bytes=24 << 20
        ),
        name="particles",
    )(
        *(
            pltpu.with_memory_space_constraint(a, pltpu.HBM)
            for a in (velocity_field, particle_state.transpose(by_row), stokes_time, box_base.T)
        ),
        live_bins,
    )
    return out.transpose(by_row)


def solution(mesh):
    placed = (
        P(None, "slab", "sub", None),
        P(("slab", "sub"), None, None),
        P(("slab", "sub"), None),
        P(("slab", "sub"), None),
        P(("slab", "sub")),
    )
    return jax.shard_map(
        body, mesh=mesh, in_specs=placed, out_specs=P(("slab", "sub"), None, None), check_vma=False
    )
```

time: 32 us -> 24.9 us (0.78)
  the two profiles are of different devices: /device:TPU:40 before, /device:TPU:2 now
where the time goes in v1:
time: 24.9 us; the launch traced here: 24.8 us
  Pallas kernels  23.5 us (94%)
  local copies, waits for them, and re-layouts  0.68 us (3%)
  between operations  0.66 us (3%)
    pallas_call x1, Pallas kernels, body(): pl.pallas_call(functools.partial(kernel, n_slab, n_sub), out_shape=jax.Sh...  23.5 us
    unnamed x1, local copies, waits for them, and re-layouts  0.68 us

profile of v1, /device:TPU:2, one launch (start us, length us, event | category | flops | bytes accessed | tf_op | source)
XLA Modules:
  0.0 24.8 jit_solution(7551039096482673874)
XLA Ops:
  0.7 23.5 %particles.1 = f32[6,32,256]{2,1,0:T(8,128)S(1)} custom-call(f32[3,16,32,512]{3,2,1,0:T(8,128)} %field.1, f32[6,32,256]{2,1,0:T(8,128)} %bitcast.4, f32[32,256]{1,0:T(8,128)} %stokes.1, s32[3,32]{1,0:T(4,128)} %bitcast.5, s32[1]{0:T(128)S(6)} %copy.7.live), custom_call_target="tpu_custom_call" | custom-call | tf_op jit(solution)/shard_map/particles/pallas_call | solution.py:213
  24.1 0.7 %copy.8 = f32[32,6,256]{2,0,1:T(8,128)} copy(f32[32,6,256]{2,0,1:T(8,128)S(1)} %bitcast.3) | data formatting | bytes 393216

commit v2 on v1

--- a/solution.py
+++ b/solution.py
@@ -65,59 +65,106 @@
 
 def kernel(n_slab, n_sub, field, states, stokes, bases_in, live, out,
            padded, parts, rates, moved, picked, planes, boxes_high, boxes_low, bases,
-           local_sems, part_sems, out_sem, send_sems, recv_sems):
-    comm = n_slab > 1
+           local_sems, part_sems, out_sem, send_sems, recv_sems, here_sem):
     _, cx, cy, nz = field.shape
     tiles = nz // LANES
     _, bins, part = states.shape
+    g, s = lax.axis_index("slab"), lax.axis_index("sub")
+
+    def at(dx, dy):
+        return (lax.rem(g + dx + n_slab, n_slab), lax.rem(s + dy + n_sub, n_sub))
+
+    left, right, down, up = at(-1, 0), at(1, 0), at(0, -1), at(0, 1)
+    odd = lax.rem(g, 2) == 1
+    even = jnp.logical_not(odd)
 
     loads = []
-    for t in range(tiles):
-        loads.append(
-            pltpu.make_async_copy(
-                field.at[:, :, :, pl.ds(t * LANES, LANES)],
-                padded.at[:, pl.ds(WIDTH, cx), t, pl.ds(TOP, cy), :],
-                local_sems.at[t],
+
+    def load(xs, ys):
+        copies = []
+        for t in range(tiles):
+            n = len(loads)
+            copy = pltpu.make_async_copy(
+                field.at[:, xs, ys, pl.ds(t * LANES, LANES)],
+                padded.at[:, shifted(xs, WIDTH), t, shifted(ys, TOP), :],
+                local_sems.at[n],
             )
+            copy.start()
+            loads.append(copy)
+            copies.append(copy)
+        return copies
+
+    def shifted(rows, by):
+        return pl.ds(rows.start + by, rows.size)
+
+    x_first, x_last, x_inner = pl.ds(0, WIDTH), pl.ds(cx - WIDTH, WIDTH), pl.ds(WIDTH, cx - 2 * WIDTH)
+    last_layers = load(x_last, pl.ds(0, cy))
+    first_layers = load(x_first, pl.ds(0, cy))
+    y_edges = load(x_inner, pl.ds(0, TOP)) + load(x_inner, pl.ds(cy - TOP, TOP))
+    rest = load(x_inner, pl.ds(TOP, cy - 2 * TOP))
+    small = []
+    for n, (here, there) in enumerate(((states, parts), (stokes, rates), (bases_in, bases))):
+        small.append(pltpu.make_async_copy(here, there, part_sems.at[n]))
+        small[-1].start()
+
+    barrier = pltpu.get_barrier_semaphore()
+    pl.semaphore_signal(barrier, inc=1, device_id=left, device_id_type=MESH)
+
+    @pl.when(odd)
+    def _():
+        for dy in (-1, 1):
+            pl.semaphore_signal(barrier, inc=1, device_id=at(-1, dy), device_id_type=MESH)
+
+    @pl.when(even)
+    def _():
+        for dy in (-1, 1):
+            pl.semaphore_signal(barrier, inc=1, device_id=at(0, dy), device_id_type=MESH)
+
+    pl.semaphore_wait(barrier, jnp.where(odd, 1, 5))
+    pl.semaphore_signal(here_sem, inc=1, device_id=right, device_id_type=MESH)
+
+    copies = []
+
+    def send(to, xs, ys, dx, dy):
+        n = len(copies)
+        copy = pltpu.make_async_remote_copy(
+            src_ref=padded.at[:, xs, :, ys, :],
+            dst_ref=padded.at[:, shifted(xs, -dx * cx), :, shifted(ys, -dy * cy), :],
+            send_sem=send_sems.at[n],
+            recv_sem=recv_sems.at[n],
+            device_id=to,
+            device_id_type=MESH,
         )
-    for n, (here, there) in enumerate(((states, parts), (stokes, rates), (bases_in, bases))):
-        loads.append(pltpu.make_async_copy(here, there, part_sems.at[n]))
-    for copy in loads:
         copy.start()
-
-    halo = []
-    if comm:
-        g, s = lax.axis_index("slab"), lax.axis_index("sub")
-        steps = [(dx, dy) for dx in (-1, 1) for dy in (-1, 1)] + [(0, -1), (0, 1), (-1, 0), (1, 0)]
-
-        def peer(dx, dy):
-            return (lax.rem(g + dx + n_slab, n_slab), lax.rem(s + dy + n_sub, n_sub))
-
-        barrier = pltpu.get_barrier_semaphore()
-        for dx, dy in steps:
-            pl.semaphore_signal(barrier, inc=1, device_id=peer(dx, dy), device_id_type=MESH)
-        pl.semaphore_wait(barrier, len(steps))
-
-        def source(d, n):
-            return {-1: (0, WIDTH), 0: (0, n), 1: (n - WIDTH, WIDTH)}[d]
-
-        def target(d, n, origin):
-            return {-1: (origin + n, WIDTH), 0: (origin, n), 1: (origin - WIDTH, WIDTH)}[d]
-
-        for k, (dx, dy) in enumerate(steps):
-            for t in range(tiles):
-                (x0, xn), (y0, yn) = source(dx, cx), source(dy, cy)
-                (u0, un), (w0, wn) = target(dx, cx, WIDTH), target(dy, cy, TOP)
-                copy = pltpu.make_async_remote_copy(
-                    src_ref=field.at[:, pl.ds(x0, xn), pl.ds(y0, yn), pl.ds(t * LANES, LANES)],
-                    dst_ref=padded.at[:, pl.ds(u0, un), t, pl.ds(w0, wn), :],
-                    send_sem=send_sems.at[k, t],
-                    recv_sem=recv_sems.at[k, t],
-                    device_id=peer(dx, dy),
-                    device_id_type=MESH,
-                )
-                copy.start()
-                halo.append(copy)
+        copies.append(copy)
+        return copy
+
+    low, high = pl.ds(TOP, WIDTH), pl.ds(TOP + cy - WIDTH, WIDTH)
+    middle = pl.ds(TOP + WIDTH, cy - 2 * WIDTH)
+
+    def send_layers(to, xs, dx):
+        corners = [send(to, xs, low, dx, 0), send(to, xs, high, dx, 0)]
+        send(to, xs, middle, dx, 0)
+        return corners
+
+    for copy in last_layers:
+        copy.wait()
+    from_left = send_layers(right, shifted(x_last, WIDTH), 1)
+    for copy in first_layers + y_edges:
+        copy.wait()
+
+    @pl.when(odd)
+    def _():
+        pl.semaphore_wait(here_sem, 1)
+
+    send(up, pl.ds(WIDTH, cx), high, 0, 1)
+    send(down, pl.ds(WIDTH, cx), low, 0, -1)
+
+    @pl.when(even)
+    def _():
+        pl.semaphore_wait(here_sem, 1)
+
+    from_right = send_layers(left, shifted(x_first, WIDTH), -1)
 
     row = lax.broadcasted_iota(jnp.int32, (LINES, LINES), 0)
     col = lax.broadcasted_iota(jnp.int32, (LINES, LINES), 1)
@@ -130,13 +177,23 @@
         power_matrix((LANES, LANES), zc // HALF % 4, zr % 4, zr // 4 == zc % HALF + q * HALF) for q in range(bins // HALF)
     ]
 
-    for copy in loads:
+    for copy in small:
         copy.wait()
     parts[0:3] = parts[0:3] - 0.5
     rates[...] = 1.0 / rates[...]
     moved[...] = parts[...]
-    for copy in halo:
+
+    for corners, xs in ((from_right, pl.ds(WIDTH + cx, WIDTH)), (from_left, pl.ds(0, WIDTH))):
+        for copy in corners:
+            copy.wait_recv()
+        send(down, xs, low, 0, -1)
+        send(up, xs, high, 0, 1)
+    for copy in rest:
         copy.wait()
+    for copy in copies:
+        copy.wait_send()
+        if not any(copy is corner for corner in from_left + from_right):
+            copy.wait_recv()
 
     lane = lax.broadcasted_iota(jnp.int32, (4, LANES), 1)
     for b in range(bins):
@@ -225,14 +282,15 @@
             pltpu.VMEM((bins // HALF, 12 * HALF, 2 * LANES), jnp.bfloat16),
             pltpu.VMEM((bins // HALF, 12 * HALF, 2 * LANES), jnp.bfloat16),
             pltpu.SMEM((3, bins), jnp.int32),
-            pltpu.SemaphoreType.DMA((tiles,)),
+            pltpu.SemaphoreType.DMA((5 * tiles,)),
             pltpu.SemaphoreType.DMA((3,)),
             pltpu.SemaphoreType.DMA,
-            pltpu.SemaphoreType.DMA((8, tiles)),
-            pltpu.SemaphoreType.DMA((8, tiles)),
+            pltpu.SemaphoreType.DMA((12,)),
+            pltpu.SemaphoreType.DMA((12,)),
+            pltpu.SemaphoreType.REGULAR,
         ],
         compiler_params=pltpu.CompilerParams(
-            collective_id=0 if n_slab > 1 else None, has_side_effects=True, vmem_limit_bytes=24 << 20
+            collective_id=0, has_side_effects=True, vmem_limit_bytes=24 << 20
         ),
         name="particles",
     )(

time: 24.9 us -> 24.2 us (0.972)
  the two profiles are of different devices: /device:TPU:2 before, /device:TPU:1 now
where the time goes in v2:
time: 24.2 us; the launch traced here: 24 us
  Pallas kernels  22.7 us (94%)
  local copies, waits for them, and re-layouts  0.68 us (3%)
  between operations  0.66 us (3%)
    pallas_call x1, Pallas kernels, body(): pl.pallas_call(functools.partial(kernel, n_slab, n_sub), out_shape=jax.Sh...  22.7 us
    unnamed x1, local copies, waits for them, and re-layouts  0.68 us

profile of v2, /device:TPU:1, one launch (start us, length us, event | category | flops | bytes accessed | tf_op | source)
XLA Modules:
  0.0 24.0 jit_solution(17659516952131961682)
XLA Ops:
  0.7 22.7 %particles.1 = f32[6,32,256]{2,1,0:T(8,128)S(1)} custom-call(f32[3,16,32,512]{3,2,1,0:T(8,128)} %field.1, f32[6,32,256]{2,1,0:T(8,128)} %bitcast.4, f32[32,256]{1,0:T(8,128)} %stokes.1, s32[3,32]{1,0:T(4,128)} %bitcast.5, s32[1]{0:T(128)S(6)} %copy.7.live), custom_call_target="tpu_custom_call" | custom-call | tf_op jit(solution)/shard_map/particles/pallas_call | solution.py:270
  23.3 0.7 %copy.8 = f32[32,6,256]{2,0,1:T(8,128)} copy(f32[32,6,256]{2,0,1:T(8,128)S(1)} %bitcast.3) | data formatting | bytes 393216

commit v3 on v2

--- a/solution.py
+++ b/solution.py
@@ -45,7 +45,7 @@
     return jnp.dot(a, b, preferred_element_type=jnp.float32)
 
 
-def sample(high_box, low_box, position):
+def sample(box, position):
     x, y, z = position
     y2, z2 = y * y, z * z
     along_z = [None, z, z2, z2 * z]
@@ -55,17 +55,19 @@
         for b in along_z:
             terms.append(jnp.ones_like(x) if a is None and b is None else a if b is None else b if a is None else a * b)
     high, low = split(jnp.concatenate(terms, axis=0))
-    slices = dot(high_box, high) + dot(low_box, high) + dot(high_box, low)
+    rows = 12 * HALF
+    both = dot(box, high)
+    slices = both[:rows] + dot(box[:rows], low) + both[rows:]
     velocity = []
     for c in range(3):
-        i = [slices[(c * 4 + i) * HALF : (c * 4 + i + 1) * HALF] for i in range(4)]
+        i = [slices[(i * 3 + c) * HALF : (i * 3 + c + 1) * HALF] for i in range(4)]
         velocity.append(((i[3] * x + i[2]) * x + i[1]) * x + i[0])
     return velocity
 
 
 def kernel(n_slab, n_sub, field, states, stokes, bases_in, live, out,
-           padded, parts, rates, moved, picked, planes, boxes_high, boxes_low, bases,
-           local_sems, part_sems, out_sem, send_sems, recv_sems, here_sem):
+           padded, parts, rates, moved, picked, planes, boxes_split, bases,
+           local_sems, part_sems, out_sem, send_sems, recv_sems, here_sems):
     _, cx, cy, nz = field.shape
     tiles = nz // LANES
     _, bins, part = states.shape
@@ -107,69 +109,118 @@
         small.append(pltpu.make_async_copy(here, there, part_sems.at[n]))
         small[-1].start()
 
+    first, second, third, last = g == 0, g == 1, g == 2, g == n_slab - 1
     barrier = pltpu.get_barrier_semaphore()
-    pl.semaphore_signal(barrier, inc=1, device_id=left, device_id_type=MESH)
-
-    @pl.when(odd)
-    def _():
-        for dy in (-1, 1):
-            pl.semaphore_signal(barrier, inc=1, device_id=at(-1, dy), device_id_type=MESH)
+
+    def tell(*offsets):
+        for dx, dy in offsets:
+            pl.semaphore_signal(barrier, inc=1, device_id=at(dx, dy), device_id_type=MESH)
+
+    tell((-1, 0))
 
     @pl.when(even)
     def _():
-        for dy in (-1, 1):
-            pl.semaphore_signal(barrier, inc=1, device_id=at(0, dy), device_id_type=MESH)
-
-    pl.semaphore_wait(barrier, jnp.where(odd, 1, 5))
-    pl.semaphore_signal(here_sem, inc=1, device_id=right, device_id_type=MESH)
+        tell((0, -1), (0, 1))
+
+    @pl.when(odd & jnp.logical_not(last))
+    def _():
+        tell((1, 0))
+
+    @pl.when(odd & jnp.logical_not(second))
+    def _():
+        tell((-1, -1), (-1, 1))
+
+    @pl.when(second)
+    def _():
+        tell((1, -1), (1, 1))
+
+    pl.semaphore_wait(barrier, jnp.where(odd, 1, jnp.where(first, 3, jnp.where(third, 8, 6))))
+
+    @pl.when(even | last)
+    def _():
+        pl.semaphore_signal(here_sems.at[0], inc=1, device_id=right, device_id_type=MESH)
+
+    @pl.when(third)
+    def _():
+        pl.semaphore_signal(here_sems.at[1], inc=1, device_id=left, device_id_type=MESH)
 
     copies = []
 
-    def send(to, xs, ys, dx, dy):
+    def remote(to, source, target):
         n = len(copies)
         copy = pltpu.make_async_remote_copy(
-            src_ref=padded.at[:, xs, :, ys, :],
-            dst_ref=padded.at[:, shifted(xs, -dx * cx), :, shifted(ys, -dy * cy), :],
+            src_ref=source,
+            dst_ref=target,
             send_sem=send_sems.at[n],
             recv_sem=recv_sems.at[n],
             device_id=to,
             device_id_type=MESH,
         )
-        copy.start()
         copies.append(copy)
         return copy
 
+    def cells(to, xs, ys, dx, dy):
+        return remote(
+            to, padded.at[:, xs, :, ys, :], padded.at[:, shifted(xs, -dx * cx), :, shifted(ys, -dy * cy), :]
+        )
+
     low, high = pl.ds(TOP, WIDTH), pl.ds(TOP + cy - WIDTH, WIDTH)
     middle = pl.ds(TOP + WIDTH, cy - 2 * WIDTH)
 
-    def send_layers(to, xs, dx):
-        corners = [send(to, xs, low, dx, 0), send(to, xs, high, dx, 0)]
-        send(to, xs, middle, dx, 0)
-        return corners
-
+    def corner_cells(to, xs, dx):
+        return [
+            remote(
+                to,
+                field.at[:, xs, ys, pl.ds(t * LANES, LANES)],
+                padded.at[:, shifted(xs, WIDTH - dx * cx), t, shifted(ys, TOP), :],
+            )
+            for ys in (pl.ds(0, WIDTH), pl.ds(cy - WIDTH, WIDTH))
+            for t in range(tiles)
+        ]
+
+    from_left, from_right = corner_cells(right, x_last, 1), corner_cells(left, x_first, -1)
+    layers_left = cells(right, shifted(x_last, WIDTH), middle, 1, 0)
+    layers_right = cells(left, shifted(x_first, WIDTH), middle, -1, 0)
+    rows_down, rows_up = cells(up, pl.ds(WIDTH, cx), high, 0, 1), cells(down, pl.ds(WIDTH, cx), low, 0, -1)
+
+    for copy in from_left:
+        copy.start()
     for copy in last_layers:
         copy.wait()
-    from_left = send_layers(right, shifted(x_last, WIDTH), 1)
-    for copy in first_layers + y_edges:
-        copy.wait()
-
-    @pl.when(odd)
-    def _():
-        pl.semaphore_wait(here_sem, 1)
-
-    send(up, pl.ds(WIDTH, cx), high, 0, 1)
-    send(down, pl.ds(WIDTH, cx), low, 0, -1)
-
-    @pl.when(even)
-    def _():
-        pl.semaphore_wait(here_sem, 1)
-
-    from_right = send_layers(left, shifted(x_first, WIDTH), -1)
+    layers_left.start()
+
+    later = first | second
+
+    @pl.when(odd & jnp.logical_not(second))
+    def _():
+        pl.semaphore_wait(here_sems.at[0], 1)
+
+    @pl.when(jnp.logical_not(later))
+    def _():
+        for copy in from_right:
+            copy.start()
+
+    for copy in first_layers:
+        copy.wait()
+
+    @pl.when(jnp.logical_not(later))
+    def _():
+        layers_right.start()
+
+    for copy in y_edges:
+        copy.wait()
+
+    @pl.when(second)
+    def _():
+        pl.semaphore_wait(here_sems.at[1], 1)
+
+    rows_down.start()
+    rows_up.start()
 
     row = lax.broadcasted_iota(jnp.int32, (LINES, LINES), 0)
     col = lax.broadcasted_iota(jnp.int32, (LINES, LINES), 1)
     along_y = power_matrix((LINES, LINES), row % 4, col % 4, row // 4 == col // 4)
-    along_x = power_matrix((LINES, LINES), row // 4 % 4, col // 4 % 4, (row // 16 == col // 16) & (row % 4 == col % 4))
+    along_x = power_matrix((LINES, LINES), row // 12, col // 12, row % 12 == col % 12)
     along_xy = exact_dot(along_x, along_y)
     zr = lax.broadcasted_iota(jnp.int32, (LANES, LANES), 0)
     zc = lax.broadcasted_iota(jnp.int32, (LANES, LANES), 1)
@@ -183,29 +234,40 @@
     rates[...] = 1.0 / rates[...]
     moved[...] = parts[...]
 
+    @pl.when(later)
+    def _():
+        pl.semaphore_wait(here_sems.at[0], 1)
+        for copy in from_right:
+            copy.start()
+        layers_right.start()
+
     for corners, xs in ((from_right, pl.ds(WIDTH + cx, WIDTH)), (from_left, pl.ds(0, WIDTH))):
         for copy in corners:
             copy.wait_recv()
-        send(down, xs, low, 0, -1)
-        send(up, xs, high, 0, 1)
+        for to, rows, dy in ((down, low, -1), (up, high, 1)):
+            cells(to, xs, rows, 0, dy).start()
     for copy in rest:
         copy.wait()
+
+    lane = lax.broadcasted_iota(jnp.int32, (4, LANES), 1)
+
+    def pick(layers):
+        for b in range(bins):
+            x0, y0, z0 = bases[0, b] + WIDTH, bases[1, b] + TOP, bases[2, b]
+            here = z0 // LANES
+            after = lax.rem(here + 1, tiles)
+            first = lane >= lax.rem(z0, LANES)
+            for i in layers:
+                for c in range(3):
+                    a = padded[c, x0 + i, here, pl.ds(y0, 4), :]
+                    n = padded[c, x0 + i, after, pl.ds(y0, 4), :]
+                    picked[b, pl.ds((i * 3 + c) * 4, 4), :] = jnp.where(first, a, n)
+
     for copy in copies:
         copy.wait_send()
         if not any(copy is corner for corner in from_left + from_right):
             copy.wait_recv()
-
-    lane = lax.broadcasted_iota(jnp.int32, (4, LANES), 1)
-    for b in range(bins):
-        x0, y0, z0 = bases[0, b] + WIDTH, bases[1, b] + TOP, bases[2, b]
-        here = z0 // LANES
-        after = lax.rem(here + 1, tiles)
-        first = lane >= lax.rem(z0, LANES)
-        for c in range(3):
-            for i in range(4):
-                a = padded[c, x0 + i, here, pl.ds(y0, 4), :]
-                n = padded[c, x0 + i, after, pl.ds(y0, 4), :]
-                picked[b, pl.ds((c * 4 + i) * 4, 4), :] = jnp.where(first, a, n)
+    pick(range(4))
 
     wide = lax.broadcasted_iota(jnp.int32, (LINES, LANES), 1)
     boxes = jnp.zeros((LINES, LANES), jnp.float32)
@@ -223,9 +285,9 @@
                 even = jnp.broadcast_to(planes[q, pl.ds(line * 4 + j, 1), :], (HALF, LANES))
                 odd = jnp.broadcast_to(planes[q, pl.ds(line * 4 + j + 1, 1), :], (HALF, LANES))
                 high, low = split(jnp.where(own, jnp.where(low_lane, even, odd), 0.0))
-                at = (q, pl.ds(line * HALF, HALF), pl.ds(side * LANES, LANES))
-                boxes_high[at] = high
-                boxes_low[at] = low
+                lanes = pl.ds(side * LANES, LANES)
+                boxes_split[q, pl.ds(line * HALF, HALF), lanes] = high
+                boxes_split[q, pl.ds((line + 12) * HALF, HALF), lanes] = low
 
     halves = range(bins // HALF)
 
@@ -234,13 +296,13 @@
         for q in halves:
             rows = pl.ds(q * HALF, HALF)
             state.append(([moved[c, rows] for c in range(3)], [moved[c + 3, rows] for c in range(3)], rates[rows]))
-        u = [sample(boxes_high[q], boxes_low[q], state[q][0]) for q in halves]
+        u = [sample(boxes_split[q], state[q][0]) for q in halves]
         mid = []
         for q in halves:
             x, v, rate = state[q]
             vm = [v[c] + (0.5 * STEP_SIZE) * (u[q][c] - v[c]) * rate for c in range(3)]
             mid.append(([x[c] + (0.5 * STEP_SIZE) * v[c] for c in range(3)], vm))
-        um = [sample(boxes_high[q], boxes_low[q], mid[q][0]) for q in halves]
+        um = [sample(boxes_split[q], mid[q][0]) for q in halves]
         for q in halves:
             rows = pl.ds(q * HALF, HALF)
             x, v, rate = state[q]
@@ -279,15 +341,14 @@
             pltpu.VMEM((6, bins, part), jnp.float32),
             pltpu.VMEM((bins, LINES, LANES), jnp.float32),
             pltpu.VMEM((bins // HALF, LINES, LANES), jnp.float32),
-            pltpu.VMEM((bins // HALF, 12 * HALF, 2 * LANES), jnp.bfloat16),
-            pltpu.VMEM((bins // HALF, 12 * HALF, 2 * LANES), jnp.bfloat16),
+            pltpu.VMEM((bins // HALF, 24 * HALF, 2 * LANES), jnp.bfloat16),
             pltpu.SMEM((3, bins), jnp.int32),
             pltpu.SemaphoreType.DMA((5 * tiles,)),
             pltpu.SemaphoreType.DMA((3,)),
             pltpu.SemaphoreType.DMA,
-            pltpu.SemaphoreType.DMA((12,)),
-            pltpu.SemaphoreType.DMA((12,)),
-            pltpu.SemaphoreType.REGULAR,
+            pltpu.SemaphoreType.DMA((4 * tiles + 8,)),
+            pltpu.SemaphoreType.DMA((4 * tiles + 8,)),
+            pltpu.SemaphoreType.REGULAR((2,)),
         ],
         compiler_params=pltpu.CompilerParams(
             collective_id=0, has_side_effects=True, vmem_limit_bytes=24 << 20

time: 24.2 us -> 22.2 us (0.917)
  the two profiles are of different devices: /device:TPU:1 before, /device:TPU:40 now
where the time goes in v3:
time: 22.2 us; the launch traced here: 22.1 us
  Pallas kernels  20.7 us (93%)
  local copies, waits for them, and re-layouts  0.68 us (3%)
  between operations  0.66 us (3%)
    pallas_call x1, Pallas kernels, body(): pl.pallas_call(functools.partial(kernel, n_slab, n_sub), out_shape=jax.Sh...  20.7 us
    unnamed x1, local copies, waits for them, and re-layouts  0.68 us

profile of v3, /device:TPU:40, one launch (start us, length us, event | category | flops | bytes accessed | tf_op | source)
XLA Modules:
  0.0 22.1 jit_solution(15876237620009287223)
XLA Ops:
  0.7 20.7 %particles.1 = f32[6,32,256]{2,1,0:T(8,128)S(1)} custom-call(f32[3,16,32,512]{3,2,1,0:T(8,128)} %field.1, f32[6,32,256]{2,1,0:T(8,128)} %bitcast.4, f32[32,256]{1,0:T(8,128)} %stokes.1, s32[3,32]{1,0:T(4,128)} %bitcast.5, s32[1]{0:T(128)S(6)} %copy.7.live), custom_call_target="tpu_custom_call" | custom-call | tf_op jit(solution)/shard_map/particles/pallas_call | solution.py:332
  21.4 0.7 %copy.8 = f32[32,6,256]{2,0,1:T(8,128)} copy(f32[32,6,256]{2,0,1:T(8,128)S(1)} %bitcast.3) | data formatting | bytes 393216

commit v4 on v3

--- a/solution.py
+++ b/solution.py
@@ -101,8 +101,8 @@
 
     x_first, x_last, x_inner = pl.ds(0, WIDTH), pl.ds(cx - WIDTH, WIDTH), pl.ds(WIDTH, cx - 2 * WIDTH)
     last_layers = load(x_last, pl.ds(0, cy))
+    y_edges = load(x_inner, pl.ds(0, TOP)) + load(x_inner, pl.ds(cy - TOP, TOP))
     first_layers = load(x_first, pl.ds(0, cy))
-    y_edges = load(x_inner, pl.ds(0, TOP)) + load(x_inner, pl.ds(cy - TOP, TOP))
     rest = load(x_inner, pl.ds(TOP, cy - 2 * TOP))
     small = []
     for n, (here, there) in enumerate(((states, parts), (stokes, rates), (bases_in, bases))):
@@ -254,9 +254,9 @@
     def pick(layers):
         for b in range(bins):
             x0, y0, z0 = bases[0, b] + WIDTH, bases[1, b] + TOP, bases[2, b]
-            here = z0 // LANES
-            after = lax.rem(here + 1, tiles)
-            first = lane >= lax.rem(z0, LANES)
+            here = lax.shift_right_logical(z0, 7)
+            after = (here + 1) & (tiles - 1)
+            first = lane >= (z0 & (LANES - 1))
             for i in layers:
                 for c in range(3):
                     a = padded[c, x0 + i, here, pl.ds(y0, 4), :]
@@ -272,7 +272,7 @@
     wide = lax.broadcasted_iota(jnp.int32, (LINES, LANES), 1)
     boxes = jnp.zeros((LINES, LANES), jnp.float32)
     for b in range(bins):
-        shift = lax.rem(4 * b + LANES - lax.rem(bases[2, b], LANES), LANES)
+        shift = (4 * b - bases[2, b]) & (LANES - 1)
         boxes = jnp.where(wide // 4 == b, pltpu.roll(picked[b], shift, 1), boxes)
     boxes = exact_dot(along_xy, boxes)
     own = lax.broadcasted_iota(jnp.int32, (HALF, LANES), 0) == lax.broadcasted_iota(jnp.int32, (HALF, LANES), 1) % HALF
@@ -312,7 +312,8 @@
                 moved[c + 3, rows] = v[c] + STEP_SIZE * (um[q][c] - vm[c]) * rate
         return carry
 
-    lax.fori_loop(0, SUBSTEPS, substep, 0)
+    for _ in range(SUBSTEPS):
+        substep(0, 0)
     keep = lax.broadcasted_iota(jnp.int32, (bins, part), 0) < live[0]
     for c in range(6):
         end = jnp.where(keep, moved[c], parts[c])

time: 22.2 us -> 21.5 us (0.968)
  Pallas kernels: 20.7 us -> 20 us
    pallas_call x1, Pallas kernels: 20.7 us -> 20 us  [body(): pl.pallas_call(functools.partial(kernel, n_slab, n_sub), out_shape=jax.Sh...]
where the time goes in v4:
time: 21.5 us; the launch traced here: 21.4 us
  Pallas kernels  20 us (93%)
  local copies, waits for them, and re-layouts  0.68 us (3%)
  between operations  0.66 us (3%)
    pallas_call x1, Pallas kernels, body(): pl.pallas_call(functools.partial(kernel, n_slab, n_sub), out_shape=jax.Sh...  20 us
    unnamed x1, local copies, waits for them, and re-layouts  0.68 us

profile of v4, /device:TPU:40, one launch (start us, length us, event | category | flops | bytes accessed | tf_op | source)
XLA Modules:
  0.0 21.4 jit_solution(16426850369775752600)
XLA Ops:
  0.7 20.0 %particles.1 = f32[6,32,256]{2,1,0:T(8,128)S(1)} custom-call(f32[3,16,32,512]{3,2,1,0:T(8,128)} %field.1, f32[6,32,256]{2,1,0:T(8,128)} %bitcast.4, f32[32,256]{1,0:T(8,128)} %stokes.1, s32[3,32]{1,0:T(4,128)} %bitcast.5, s32[1]{0:T(128)S(6)} %copy.7.live), custom_call_target="tpu_custom_call" | custom-call | tf_op jit(solution)/shard_map/particles/pallas_call | solution.py:333
  20.7 0.7 %copy.8 = f32[32,6,256]{2,0,1:T(8,128)} copy(f32[32,6,256]{2,0,1:T(8,128)S(1)} %bitcast.3) | data formatting | bytes 393216

commit v5 on v4

--- a/solution.py
+++ b/solution.py
@@ -116,7 +116,9 @@
         for dx, dy in offsets:
             pl.semaphore_signal(barrier, inc=1, device_id=at(dx, dy), device_id_type=MESH)
 
-    tell((-1, 0))
+    @pl.when(jnp.logical_not(first))
+    def _():
+        tell((-1, 0))
 
     @pl.when(even)
     def _():
@@ -135,6 +137,10 @@
         tell((1, -1), (1, 1))
 
     pl.semaphore_wait(barrier, jnp.where(odd, 1, jnp.where(first, 3, jnp.where(third, 8, 6))))
+
+    @pl.when(first)
+    def _():
+        tell((-1, 0))
 
     @pl.when(even | last)
     def _():
@@ -179,9 +185,22 @@
         ]
 
     from_left, from_right = corner_cells(right, x_last, 1), corner_cells(left, x_first, -1)
+    across = [
+        remote(
+            at(1, 1),
+            field.at[:, x_last, pl.ds(cy - WIDTH, WIDTH), pl.ds(t * LANES, LANES)],
+            padded.at[:, pl.ds(0, WIDTH), t, pl.ds(TOP - WIDTH, WIDTH), :],
+        )
+        for t in range(tiles)
+    ]
     layers_left = cells(right, shifted(x_last, WIDTH), middle, 1, 0)
     layers_right = cells(left, shifted(x_first, WIDTH), middle, -1, 0)
     rows_down, rows_up = cells(up, pl.ds(WIDTH, cx), high, 0, 1), cells(down, pl.ds(WIDTH, cx), low, 0, -1)
+
+    @pl.when(last)
+    def _():
+        for copy in across:
+            copy.start()
 
     for copy in from_left:
         copy.start()
@@ -244,8 +263,16 @@
     for corners, xs in ((from_right, pl.ds(WIDTH + cx, WIDTH)), (from_left, pl.ds(0, WIDTH))):
         for copy in corners:
             copy.wait_recv()
-        for to, rows, dy in ((down, low, -1), (up, high, 1)):
-            cells(to, xs, rows, 0, dy).start()
+        cells(down, xs, low, 0, -1).start()
+        onward = cells(up, xs, high, 0, 1)
+        if corners is from_right:
+            onward.start()
+            continue
+
+        @pl.when(jnp.logical_not(first))
+        def _():
+            onward.start()
+
     for copy in rest:
         copy.wait()
 
@@ -264,9 +291,25 @@
                     picked[b, pl.ds((i * 3 + c) * 4, 4), :] = jnp.where(first, a, n)
 
     for copy in copies:
-        copy.wait_send()
-        if not any(copy is corner for corner in from_left + from_right):
+        if not any(copy is other for other in across + [onward]):
+            copy.wait_send()
+            if not any(copy is corner for corner in from_left + from_right):
+                copy.wait_recv()
+
+    @pl.when(last)
+    def _():
+        for copy in across:
+            copy.wait_send()
+
+    @pl.when(first)
+    def _():
+        for copy in across:
             copy.wait_recv()
+
+    @pl.when(jnp.logical_not(first))
+    def _():
+        onward.wait()
+
     pick(range(4))
 
     wide = lax.broadcasted_iota(jnp.int32, (LINES, LANES), 1)
@@ -347,8 +390,8 @@
             pltpu.SemaphoreType.DMA((5 * tiles,)),
             pltpu.SemaphoreType.DMA((3,)),
             pltpu.SemaphoreType.DMA,
-            pltpu.SemaphoreType.DMA((4 * tiles + 8,)),
-            pltpu.SemaphoreType.DMA((4 * tiles + 8,)),
+            pltpu.SemaphoreType.DMA((5 * tiles + 8,)),
+            pltpu.SemaphoreType.DMA((5 * tiles + 8,)),
             pltpu.SemaphoreType.REGULAR((2,)),
         ],
         compiler_params=pltpu.CompilerParams(

time: 21.5 us -> 21 us (0.977)
  the two profiles are of different devices: /device:TPU:40 before, /device:TPU:30 now
where the time goes in v5:
time: 21 us; the launch traced here: 20.9 us
  Pallas kernels  19.5 us (93%)
  local copies, waits for them, and re-layouts  0.68 us (3%)
  between operations  0.66 us (3%)
    pallas_call x1, Pallas kernels, body(): pl.pallas_call(functools.partial(kernel, n_slab, n_sub), out_shape=jax.Sh...  19.5 us
    unnamed x1, local copies, waits for them, and re-layouts  0.68 us

profile of v5, /device:TPU:30, one launch (start us, length us, event | category | flops | bytes accessed | tf_op | source)
XLA Modules:
  0.0 20.9 jit_solution(2237609300422684432)
XLA Ops:
  0.7 19.5 %particles.1 = f32[6,32,256]{2,1,0:T(8,128)S(1)} custom-call(f32[3,16,32,512]{3,2,1,0:T(8,128)} %field.1, f32[6,32,256]{2,1,0:T(8,128)} %bitcast.4, f32[32,256]{1,0:T(8,128)} %stokes.1, s32[3,32]{1,0:T(4,128)} %bitcast.5, s32[1]{0:T(128)S(6)} %copy.7.live), custom_call_target="tpu_custom_call" | custom-call | tf_op jit(solution)/shard_map/particles/pallas_call | solution.py:376
  20.2 0.7 %copy.8 = f32[32,6,256]{2,0,1:T(8,128)} copy(f32[32,6,256]{2,0,1:T(8,128)S(1)} %bitcast.3) | data formatting | bytes 393216

commit v6 on v5

--- a/solution.py
+++ b/solution.py
@@ -195,7 +195,10 @@
     ]
     layers_left = cells(right, shifted(x_last, WIDTH), middle, 1, 0)
     layers_right = cells(left, shifted(x_first, WIDTH), middle, -1, 0)
-    rows_down, rows_up = cells(up, pl.ds(WIDTH, cx), high, 0, 1), cells(down, pl.ds(WIDTH, cx), low, 0, -1)
+    rows_down, rows_up = (
+        [cells(to, pl.ds(x, n), rows, 0, dy) for x, n in ((2 * WIDTH, cx - WIDTH), (WIDTH, WIDTH))]
+        for to, rows, dy in ((up, high, 1), (down, low, -1))
+    )
 
     @pl.when(last)
     def _():
@@ -219,22 +222,23 @@
         for copy in from_right:
             copy.start()
 
+    for copy in y_edges:
+        copy.wait()
+
+    @pl.when(second)
+    def _():
+        pl.semaphore_wait(here_sems.at[1], 1)
+
+    rows_down[0].start()
+    rows_up[0].start()
     for copy in first_layers:
         copy.wait()
+    rows_down[1].start()
+    rows_up[1].start()
 
     @pl.when(jnp.logical_not(later))
     def _():
         layers_right.start()
-
-    for copy in y_edges:
-        copy.wait()
-
-    @pl.when(second)
-    def _():
-        pl.semaphore_wait(here_sems.at[1], 1)
-
-    rows_down.start()
-    rows_up.start()
 
     row = lax.broadcasted_iota(jnp.int32, (LINES, LINES), 0)
     col = lax.broadcasted_iota(jnp.int32, (LINES, LINES), 1)
@@ -390,8 +394,8 @@
             pltpu.SemaphoreType.DMA((5 * tiles,)),
             pltpu.SemaphoreType.DMA((3,)),
             pltpu.SemaphoreType.DMA,
-            pltpu.SemaphoreType.DMA((5 * tiles + 8,)),
-            pltpu.SemaphoreType.DMA((5 * tiles + 8,)),
+            pltpu.SemaphoreType.DMA((5 * tiles + 10,)),
+            pltpu.SemaphoreType.DMA((5 * tiles + 10,)),
             pltpu.SemaphoreType.REGULAR((2,)),
         ],
         compiler_params=pltpu.CompilerParams(

time: 21 us -> 21 us (level)
  no operation moved by 1% of the time
where the time goes in v6:
time: 21 us; the launch traced here: 20.9 us
  Pallas kernels  19.6 us (93%)
  local copies, waits for them, and re-layouts  0.68 us (3%)
  between operations  0.66 us (3%)
    pallas_call x1, Pallas kernels, body(): pl.pallas_call(functools.partial(kernel, n_slab, n_sub), out_shape=jax.Sh...  19.6 us
    unnamed x1, local copies, waits for them, and re-layouts  0.68 us

profile of v6, /device:TPU:30, one launch (start us, length us, event | category | flops | bytes accessed | tf_op | source)
XLA Modules:
  0.0 20.9 jit_solution(18424160407666206351)
XLA Ops:
  0.7 19.6 %particles.1 = f32[6,32,256]{2,1,0:T(8,128)S(1)} custom-call(f32[3,16,32,512]{3,2,1,0:T(8,128)} %field.1, f32[6,32,256]{2,1,0:T(8,128)} %bitcast.4, f32[32,256]{1,0:T(8,128)} %stokes.1, s32[3,32]{1,0:T(4,128)} %bitcast.5, s32[1]{0:T(128)S(6)} %copy.7.live), custom_call_target="tpu_custom_call" | custom-call | tf_op jit(solution)/shard_map/particles/pallas_call | solution.py:380
  20.2 0.7 %copy.8 = f32[32,6,256]{2,0,1:T(8,128)} copy(f32[32,6,256]{2,0,1:T(8,128)S(1)} %bitcast.3) | data formatting | bytes 393216
